TPU v7x, 128 devices: a whole 4x4x4 slice. The times are simulated.
128 devices in a mesh: chan: 8 (over y, core), facet: 16 (over z, x).
Axes of the slice: x: 4, y: 4, z: 4, core: 2. Of those that a mesh axis runs over, the one named last changes fastest.
Arguments:
- visibilities: bfloat16 [32, 8, 8, 65536], P(None, None, 'chan', 'facet'), may hold values from -6 to 6
- w_kernel: bfloat16 [32, 2, 8], replicated, may hold values from -2 to 2
- w_index: int32 [8, 65536], P(None, 'facet'), may hold values from 0 to 31
- cell_offsets: int32 [2, 8, 65536], P(None, None, 'facet'), may hold values from 0 to 24
- block_sub: int32 [8, 128], P(None, 'facet'), may hold values from 0 to 31
- intersection_rows: int32 [16, 32], replicated, may hold values from 0 to 63, as said below
- intersection_count: int32 [16], replicated, may hold values from 1 to 32, as said below
Outputs:
- sky_image: float32 [32, 4, 64, 32768], P('chan', None, None, 'facet')
Inputs may be any that keep to these rules, and one draw needn't show every extreme that they name: `intersection_rows`: the rows in one facet's list are distinct. `intersection_count`: some facet other than the last has exactly 32 entries in use.
All inputs are finite; a program needn't handle non-finite values.
Results may differ from a plain program's by a relative error of at most 0.0059.
Values may be sent and summed in bfloat16 or wider, within the bound.
A program may use at most 128 MiB of HBM per device.

v0:
```python
import math
import jax
import jax.numpy as jnp
from jax import lax
from jax.sharding import PartitionSpec as P

BLK = 512
SG = 32
NSUB = 32
FX = 2048
FY = 64
MARGIN = 128


def shifted(block, axis, distance):
    devices = range(lax.axis_size(axis))
    route = [(i - distance, i) for i in devices if i - distance in devices]
    return lax.ppermute(block, axis, route)


def anchors(sub_index, side_len, period):
    span = period // side_len
    row_anchor = (jnp.mod(sub_index * 37, span) - span // 2) * side_len
    col_anchor = (jnp.mod(sub_index * 53 + 5, span) - span // 2) * side_len
    return (row_anchor, col_anchor)


def row_tables(sub_index, side_len, height, period):
    row_anchor, col_anchor = anchors(sub_index, side_len, period)
    cell_ids = jnp.arange(side_len, dtype=jnp.int32)
    line_ids = jnp.arange(height, dtype=jnp.int32) - height // 2
    phase_int = (row_anchor[:, None, None] + cell_ids[None, None, :]) * line_ids[None, :, None]
    radians = jnp.mod(phase_int, period).astype(jnp.float32) * (2.0 * math.pi / period)
    return (jnp.cos(radians).astype(jnp.bfloat16), jnp.sin(radians).astype(jnp.bfloat16))


def col_tables(sub_index, side_len, col_ids, period):
    row_anchor, col_anchor = anchors(sub_index, side_len, period)
    cell_ids = jnp.arange(side_len, dtype=jnp.int32)
    phase_int = (col_anchor[:, None, None] + cell_ids[None, :, None]) * (col_ids - period // 2)[
        None, None, :
    ]
    radians = jnp.mod(phase_int, period).astype(jnp.float32) * (2.0 * math.pi / period)
    return (jnp.cos(radians).astype(jnp.bfloat16), (-jnp.sin(radians)).astype(jnp.bfloat16))


def place_kernel(values, offsets, side_len):
    distance = jnp.arange(side_len, dtype=jnp.int32)[:, None] - offsets[None, :]
    running = jnp.zeros((values.shape[0], side_len, offsets.shape[0]), jnp.float32)
    for tap_idx in range(values.shape[1]):
        running = (
            running + values[:, tap_idx, None, :] * (distance == tap_idx).astype(jnp.float32)[None]
        )
    return running


def combine(products, side_len, row_width):
    real_part = products[:, :side_len, :row_width] - products[:, side_len:, row_width:]
    imag_part = products[:, :side_len, row_width:] + products[:, side_len:, :row_width]
    return jnp.stack([real_part, imag_part], axis=1)


def block_terms(vis_part, plane_ids, cell_pos, kernel, side_len, block_len):
    planes = kernel.shape[0]
    plane_pick = (jnp.arange(planes, dtype=jnp.int32)[:, None] == plane_ids[None, :]).astype(
        jnp.float32
    )
    values = jnp.einsum(
        "wqk,wr->qkr", kernel.astype(jnp.float32), plane_pick, precision=lax.Precision.HIGHEST
    )
    left_kern = place_kernel(values, cell_pos[0], side_len).astype(jnp.bfloat16)
    right_kern = place_kernel(values, cell_pos[1], side_len)
    num_pols = vis_part.shape[1] // 2
    vis_real = vis_part[:, :num_pols].astype(jnp.float32)[:, :, None, :]
    vis_imag = vis_part[:, num_pols:].astype(jnp.float32)[:, :, None, :]
    y_real = (vis_real * right_kern[0][None, None] - vis_imag * right_kern[1][None, None]).astype(
        jnp.bfloat16
    )
    y_imag = (vis_real * right_kern[1][None, None] + vis_imag * right_kern[0][None, None]).astype(
        jnp.bfloat16
    )
    num_rows = plane_ids.shape[0]
    blocks = num_rows // block_len
    row_width = vis_part.shape[0] * num_pols * side_len
    stacked = jnp.concatenate(
        [
            y_real.reshape(row_width, blocks, block_len),
            y_imag.reshape(row_width, blocks, block_len),
        ],
        axis=0,
    )
    left_flat = left_kern.reshape(2 * side_len, blocks, block_len)
    products = lax.dot_general(
        left_flat, stacked, (((2,), (2,)), ((1,), (1,))), preferred_element_type=jnp.float32
    )
    return combine(products, side_len, row_width)


def to_rows(subgrid, row_cos, row_sin, img_scale):
    sub_real = subgrid[:, 0]
    sub_imag = subgrid[:, 1]

    def apply_table(table, data):
        return jnp.einsum("gyu,guq->gyq", table, data, preferred_element_type=jnp.float32)

    real_part = apply_table(row_cos, sub_real) - apply_table(row_sin, sub_imag)
    imag_part = apply_table(row_cos, sub_imag) + apply_table(row_sin, sub_real)
    return (jnp.stack([real_part, imag_part], axis=1) * img_scale).astype(jnp.bfloat16)


def project(image_sum, row_image, first_sub, col_ids, period):
    num_items = row_image.shape[0]
    group_len = math.gcd(num_items, 8)
    side_len = SG
    mixed = image_sum.shape[0]
    shaped = row_image.reshape(num_items, 2, row_image.shape[2], mixed, side_len)

    def add_group(turn_idx, running):
        row_piece = lax.dynamic_slice_in_dim(shaped, turn_idx * group_len, group_len, 0)
        sub_index = first_sub + turn_idx * group_len + jnp.arange(group_len, dtype=jnp.int32)
        col_cos, col_sin = col_tables(sub_index, side_len, col_ids, period)
        col_table = jnp.stack([col_cos, col_sin], axis=1)
        return running + jnp.einsum(
            "grycv,grvx->cyx", row_piece, col_table, preferred_element_type=jnp.float32
        )

    return lax.fori_loop(0, num_items // group_len, add_group, image_sum)


def shards(
    visibilities, w_kernel, w_index, cell_offsets, block_sub, intersection_rows, intersection_count
):
    turned = lax.all_to_all(visibilities, "chan", split_axis=0, concat_axis=2, tiled=True)
    groups = lax.axis_size("chan")
    facets = lax.axis_size("facet")
    num_chans = turned.shape[0]
    num_pols = turned.shape[1] // 2
    side_len = SG
    per_dev = w_index.shape[1] // BLK
    row_width = num_chans * num_pols * side_len

    def grid_group(group_id):
        vis_part = lax.dynamic_index_in_dim(turned, group_id, 2, keepdims=False)
        plane_ids = lax.dynamic_index_in_dim(w_index, group_id, 0, keepdims=False)
        cell_pos = lax.dynamic_index_in_dim(cell_offsets, group_id, 1, keepdims=False)
        return block_terms(vis_part, plane_ids, cell_pos, w_kernel, side_len, BLK)

    grid_parts = lax.map(grid_group, jnp.arange(groups, dtype=jnp.int32))
    blocks = groups * per_dev
    grid_parts = grid_parts.reshape(blocks, 2 * side_len * row_width)
    sub_ids = block_sub.reshape(blocks)
    plane_pick = (jnp.arange(NSUB, dtype=jnp.int32)[:, None] == sub_ids[None, :]).astype(
        jnp.float32
    )
    img_scale = 1.0 / math.sqrt(groups * facets * w_index.shape[1])
    period = FX * facets
    facet_id = lax.axis_index("facet")
    col_ids = facet_id * FX + jnp.arange(FX, dtype=jnp.int32)
    image = jnp.zeros((num_chans * num_pols, FY, FX), jnp.float32)
    partial_sum = jnp.dot(plane_pick, grid_parts, precision=lax.Precision.HIGHEST)
    summed = lax.psum(partial_sum, "facet")
    subgrid = summed.reshape(NSUB, 2, side_len, row_width).astype(jnp.bfloat16)
    sub_index = jnp.arange(NSUB, dtype=jnp.int32)
    row_cos, row_sin = row_tables(sub_index, side_len, FY, period)
    row_image = to_rows(subgrid, row_cos, row_sin, img_scale)
    image = project(image, row_image, 0, col_ids, period)
    line_ids = jnp.arange(FY, dtype=jnp.int32)
    slot_ids = jnp.arange(intersection_rows.shape[1], dtype=jnp.int32)
    edge_cols = image[:, :, FX - MARGIN :]
    listed = lax.dynamic_index_in_dim(intersection_rows, facet_id, 0, keepdims=False)
    in_use = lax.dynamic_index_in_dim(intersection_count, facet_id, 0, keepdims=False)
    row_keep = jnp.sum(
        ((listed[:, None] == line_ids[None, :]) & (slot_ids[:, None] < in_use)).astype(jnp.float32),
        axis=0,
    )
    arrived = shifted(edge_cols * row_keep[None, :, None], "facet", 1)
    sky_image = jnp.concatenate([image[:, :, :MARGIN] + arrived, image[:, :, MARGIN:]], axis=2)
    return sky_image.reshape(num_chans, num_pols, FY, FX)


def solution(mesh):
    return jax.shard_map(
        shards,
        mesh=mesh,
        in_specs=(
            P(None, None, "chan", "facet"),
            P(),
            P(None, "facet"),
            P(None, None, "facet"),
            P(None, "facet"),
            P(),
            P(),
        ),
        out_specs=P("chan", None, None, "facet"),
        check_vma=False,
    )
```

profile of v0, /device:TPU:2, one launch (start us, length us, event | category | flops | bytes accessed | tf_op | source)
XLA Modules:
  0.0 462.6 jit_solution(6023699204950626542)
XLA Ops:
  0.0 4.6 all-to-all-start
  6.7 25.1 %all-to-all-done = bf16[32,8,1,4096]{3,1,2,0:T(8,128)(2,1)S(1)} async-done(((bf16[32,8,1,4096]{3,1,2,0:T(8,128)(2,1)}), bf16[32,8,1,4096]{3,1,2,0:T(8,128)(2,1)S(1)}, u32[]{:S(2)}, u32[]{:S(2)}) %all-to-all-start) | async-done | bytes 2097184 | tf_op jit(solution)/shard_map/all_to_all | solution.py:133
  31.8 175.5 %while.27 = (s32[]{:T(128)}, f32[8,8,2,32,512]{4,3,2,1,0:T(8,128)}, s32[8]{0:T(128)S(1)}, s32[8,4096]{1,0:T(8,128)}, bf16[32,2,8]{0,2,1:T(8,128)(2,1)S(1)}, /*in...) while((s32[]{:T(128)}, f32[8,8,2,32,512]{4,3,2,1,0:T(8,128)}, ...), condition=%wide.region_1.2_spmd, body=%wide.region_0.1_spmd.sunk | while | flops 587988992 | bytes 84559040 | solution.py:148
  207.4 9.4 %reshape.590 = f32[64,32768]{1,0:T(8,128)} reshape(f32[8,8,2,32,512]{4,3,2,1,0:T(8,128)} %get-tuple-element.178) | data formatting | bytes 16777216 | tf_op jit(solution)/shard_map/reshape | solution.py:150
  216.7 8.4 %fusion.60 = f32[32,32768]{1,0:T(8,128)} fusion(f32[64,32768]{1,0:T(8,128)} %reshape.590, s32[64]{0:T(128)S(1)} %eq.182), kind=kOutput, calls=%fused_computation.121 | convolution fusion | flops 805308416 | bytes 12583168 | tf_op jit(solution)/shard_map/dot_general | solution.py:160
  225.1 103.7 %all-reduce.1 = bf16[32,32768]{1,0:T(8,128)(2,1)} all-reduce(f32[32,32768]{1,0:T(8,128)} %fusion.60), channel_id=1, replica_groups=mesh['chan'=8,'facet'=16] {'facet'}, use_global_device_ids=true, to_apply=%region_2.3 | all-reduce | flops 1048576 | bytes 6291456 | tf_op jit(solution)/shard_map/psum | solution.py:161
  333.9 4.1 fusion.55
  337.9 4.2 convolution_add_fusion
  342.1 6.8 %copy.38 = f32[32,64,512]{1,2,0:T(8,128)} copy(f32[32,64,512]{2,1,0:T(8,128)} %convolution_add_fusion) | data formatting | bytes 8388608 | tf_op jit(solution)/shard_map/add | solution.py:107
  349.0 5.7 %convolution_subtract_fusion = f32[32,64,512]{2,1,0:T(8,128)} fusion(f32[32,64,512]{2,1,0:T(8,128)} %fusion.55, bf16[32,2,32,512]{3,2,1,0:T(8,128)(2,1)S(1)} %bitcast.145, s32[64]{0:T(128)S(1)} %iota_add_fusion.2, s32[32,32]{1,0:T(8,128)S(1)} %iota_add_fusion.1), kind=kOutput, calls=%fused_computation.100 | convolution fusion | flops 69140480 | bytes 9454080 | tf_op jit(solution)/shard_map/gyu,guq->gyq/dot_general | solution.py:104
  354.7 6.9 %copy.37 = f32[32,64,512]{1,2,0:T(8,128)} copy(f32[32,64,512]{2,1,0:T(8,128)} %convolution_subtract_fusion) | data formatting | bytes 8388608 | tf_op jit(solution)/shard_map/sub | solution.py:106
  361.6 9.8 %fusion.54 = bf16[32,2,64,16,32]{2,4,3,0,1:T(8,128)(2,1)} fusion(f32[32,1,64,16,32]{2,4,3,0,1:T(8,128)} %bitcast.140, f32[32,1,64,16,32]{2,4,3,0,1:T(8,128)} %bitcast.141), kind=kLoop, calls=%fused_computation.97 | loop fusion | flops 6291456 | bytes 12582912 | tf_op jit(solution)/shard_map/convert_element_type | solution.py:108
  371.5 73.2 %while.28 = (s32[]{:T(128)}, f32[16,64,2048]{2,1,0:T(8,128)}, bf16[32,2,64,16,32]{2,4,3,0,1:T(8,128)(2,1)}, s32[]{:T(128)}, s32[]{:T(128)}, /*index=5*/s32[]{:T(128)}, s32[]{:T(128)}, s32[]{:T(128)}) while((s32[]{:T(128)}, f32[16,64,2048]{2,1,0:T(8,128)}, bf16[32,2,64,16,32]{2,4,3,0,1:T(8,128)(2,1)}, s32[]{:T(128)}, s32[]{:T(128)}, ...), condition=%wide.region_4.5_spmd.clone, body=%wide.region_3.4_spmd.clone.sunk | while | flops 2164789760 | bytes 23087328 | solution.py:127
  371.5 8.9 %cosine_convert_fusion.5 = (bf16[8,1,32,2048]{3,2,1,0:T(8,128)(2,1)S(1)}, bf16[8,1,32,2048]{3,2,1,0:T(8,128)(2,1)S(1)}) fusion(s32[2048]{0:T(1024)S(1)} %add_add_fusion.2, s32[8,32]{1,0:T(8,128)S(1)} %iota_add_fusion.4), kind=kLoop, calls=%fused_computation.85.clone.1 | loop fusion | flops 8912896 | bytes 2106368 | tf_op jit(solution)/shard_map/while/body/eval_jaxpr/convert_element_type | solution.py:44
  380.5 7.4 %bitcast_add_fusion.2 = f32[16,64,2048]{2,1,0:T(8,128)} fusion(f32[16,64,2048]{2,1,0:T(8,128)} %get-tuple-element.474, pred[]{:T(512)S(6)} %compare.19, bf16[8,1,32,2048]{3,2,1,0:T(8,128)(2,1)S(1)} %get-tuple-element.430, bf16[8,1,32,2048]{3,2,1,0:T(8,128)(2,1)S(1)} %get-tuple-element.431, bf16[32,2,64,16,32]{2,4,3,0,1:T(8,128)(2,1)} %get-tuple-element.483, ...), kind=kOutput, calls=%fused_computation.71.clone.1 | convolution fusion | flops 2155872256 | bytes 20971524 | tf_op jit(solution)/shard_map/while/body/eval_jaxpr/grycv,grvx->cyx/dot_general | solution.py:123
  388.0 8.9 %cosine_convert_fusion.5 = (bf16[8,1,32,2048]{3,2,1,0:T(8,128)(2,1)S(1)}, bf16[8,1,32,2048]{3,2,1,0:T(8,128)(2,1)S(1)}) fusion(s32[2048]{0:T(1024)S(1)} %add_add_fusion.2, s32[8,32]{1,0:T(8,128)S(1)} %iota_add_fusion.4), kind=kLoop, calls=%fused_computation.85.clone.1 | loop fusion | flops 8912896 | bytes 2106368 | tf_op jit(solution)/shard_map/while/body/eval_jaxpr/convert_element_type | solution.py:44
  397.0 9.9 %bitcast_add_fusion.2 = f32[16,64,2048]{2,1,0:T(8,128)} fusion(f32[16,64,2048]{2,1,0:T(8,128)} %get-tuple-element.474, pred[]{:T(512)S(6)} %compare.19, bf16[8,1,32,2048]{3,2,1,0:T(8,128)(2,1)S(1)} %get-tuple-element.430, bf16[8,1,32,2048]{3,2,1,0:T(8,128)(2,1)S(1)} %get-tuple-element.431, bf16[32,2,64,16,32]{2,4,3,0,1:T(8,128)(2,1)} %get-tuple-element.483, ...), kind=kOutput, calls=%fused_computation.71.clone.1 | convolution fusion | flops 2155872256 | bytes 20971524 | tf_op jit(solution)/shard_map/while/body/eval_jaxpr/grycv,grvx->cyx/dot_general | solution.py:123
  406.9 8.9 %cosine_convert_fusion.5 = (bf16[8,1,32,2048]{3,2,1,0:T(8,128)(2,1)S(1)}, bf16[8,1,32,2048]{3,2,1,0:T(8,128)(2,1)S(1)}) fusion(s32[2048]{0:T(1024)S(1)} %add_add_fusion.2, s32[8,32]{1,0:T(8,128)S(1)} %iota_add_fusion.4), kind=kLoop, calls=%fused_computation.85.clone.1 | loop fusion | flops 8912896 | bytes 2106368 | tf_op jit(solution)/shard_map/while/body/eval_jaxpr/convert_element_type | solution.py:44
  415.9 9.9 %bitcast_add_fusion.2 = f32[16,64,2048]{2,1,0:T(8,128)} fusion(f32[16,64,2048]{2,1,0:T(8,128)} %get-tuple-element.474, pred[]{:T(512)S(6)} %compare.19, bf16[8,1,32,2048]{3,2,1,0:T(8,128)(2,1)S(1)} %get-tuple-element.430, bf16[8,1,32,2048]{3,2,1,0:T(8,128)(2,1)S(1)} %get-tuple-element.431, bf16[32,2,64,16,32]{2,4,3,0,1:T(8,128)(2,1)} %get-tuple-element.483, ...), kind=kOutput, calls=%fused_computation.71.clone.1 | convolution fusion | flops 2155872256 | bytes 20971524 | tf_op jit(solution)/shard_map/while/body/eval_jaxpr/grycv,grvx->cyx/dot_general | solution.py:123
  425.8 8.9 %cosine_convert_fusion.5 = (bf16[8,1,32,2048]{3,2,1,0:T(8,128)(2,1)S(1)}, bf16[8,1,32,2048]{3,2,1,0:T(8,128)(2,1)S(1)}) fusion(s32[2048]{0:T(1024)S(1)} %add_add_fusion.2, s32[8,32]{1,0:T(8,128)S(1)} %iota_add_fusion.4), kind=kLoop, calls=%fused_computation.85.clone.1 | loop fusion | flops 8912896 | bytes 2106368 | tf_op jit(solution)/shard_map/while/body/eval_jaxpr/convert_element_type | solution.py:44
  434.8 9.9 %bitcast_add_fusion.2 = f32[16,64,2048]{2,1,0:T(8,128)} fusion(f32[16,64,2048]{2,1,0:T(8,128)} %get-tuple-element.474, pred[]{:T(512)S(6)} %compare.19, bf16[8,1,32,2048]{3,2,1,0:T(8,128)(2,1)S(1)} %get-tuple-element.430, bf16[8,1,32,2048]{3,2,1,0:T(8,128)(2,1)S(1)} %get-tuple-element.431, bf16[32,2,64,16,32]{2,4,3,0,1:T(8,128)(2,1)} %get-tuple-element.483, ...), kind=kOutput, calls=%fused_computation.71.clone.1 | convolution fusion | flops 2155872256 | bytes 20971524 | tf_op jit(solution)/shard_map/while/body/eval_jaxpr/grycv,grvx->cyx/dot_general | solution.py:123
  447.7 3.8 slice.85
  451.5 5.3 %collective-permute-done = f32[16,64,128]{2,1,0:T(8,128)S(1)} collective-permute-done((f32[16,64,128]{2,1,0:T(8,128)S(1)}, f32[16,64,128]{2,1,0:T(8,128)S(1)}, u32[]{:S(2)}, u32[]{:S(2)}) %collective-permute-start) | collective-permute-done | bytes 524320 | tf_op jit(solution)/shard_map/ppermute | solution.py:18
  458.0 4.6 pad_maximum_fusion
  (240 shorter events, 170.8 us)
Async XLA Ops:
  0.0 6.0 %copy-start = (s32[16,32]{1,0:T(8,128)S(1)}, s32[16,32]{1,0:T(8,128)}, u32[]{:S(2)}) copy-start(s32[16,32]{1,0:T(8,128)} %param.16) | copy-start | bytes 6148
  0.0 4.6 %copy-start.3 = (s32[8,8]{1,0:T(8,128)S(1)}, s32[8,8]{1,0:T(8,128)}, u32[]{:S(2)}) copy-start(s32[8,8]{1,0:T(8,128)} %param.15) | copy-start | bytes 772
  0.0 4.7 %copy-start.5 = (s32[16]{0:T(128)S(1)}, s32[16]{0:T(128)}, u32[]{:S(2)}) copy-start(s32[16]{0:T(128)} %param.17) | copy-start | bytes 196
  0.0 31.8 %copy-start.2 = (bf16[32,2,8]{0,2,1:T(8,128)(2,1)S(1)}, bf16[32,2,8]{0,2,1:T(8,128)(2,1)}, u32[]{:S(2)}) copy-start(bf16[32,2,8]{0,2,1:T(8,128)(2,1)} %param.12) | copy-start | bytes 3076
  0.0 31.8 %all-to-all-start = ((bf16[32,8,1,4096]{3,1,2,0:T(8,128)(2,1)}), bf16[32,8,1,4096]{3,1,2,0:T(8,128)(2,1)S(1)}, u32[]{:S(2)}, u32[]{:S(2)}) async-start(bf16[32,8,1,4096]{3,1,2,0:T(8,128)(2,1)} %param.11), calls=%async_computation | async-start | bytes 4194304 | tf_op jit(solution)/shard_map/all_to_all | solution.py:133
  371.5 73.2 %copy-start.4 = (f32[64]{0:T(128)S(1)}, f32[64]{0:T(128)}, u32[]{:S(2)}) copy-start(f32[64]{0:T(128)} %convert_reduce_fusion) | copy-start | bytes 772
  445.8 11.1 %collective-permute-start = (f32[16,64,128]{2,1,0:T(8,128)S(1)}, f32[16,64,128]{2,1,0:T(8,128)S(1)}, u32[]{:S(2)}, u32[]{:S(2)}) collective-permute-start(f32[16,64,128]{2,1,0:T(8,128)S(1)} %slice_multiply_fusion), channel_id=1, source_target_pairs={{0,1},{1,2},{2,3},{3,4},{4,5},{5,6},{6,7},{7,8},{8,9},{9,10},{10,1... | collective-permute-start | bytes 1572872 | tf_op jit(solution)/shard_map/ppermute | solution.py:18
  458.0 4.6 copy-start.1
where the time goes:
time: 464 us; the launch traced here: 463 us
  local copies, waits for them, and re-layouts  115 us (25%)
  blocking collectives  104 us (22%)
  other arithmetic  102 us (22%)
  matrix products  88.1 us (19%)
  waiting for transfers between devices  30.5 us (7%)
  loops' own time  16.5 us (4%)
  starting transfers between devices  6.53 us (1%)
    psum x1, blocking collectives, shards(): summed = lax.psum(partial_sum, 'facet')  104 us
    while x56, local copies, waits for them, and re-layouts  38.8 us
    dot_general x4, matrix products, add_group(): jnp.einsum('grycv,grvx->cyx', row_piece, col_table, preferred_element_typ...  37.1 us
    convert_element_type x4, other arithmetic, col_tables(): jnp.cos(radians).astype(jnp.bfloat16)  35.7 us
    all_to_all x1, waiting for transfers between devices, shards(): lax.all_to_all(visibilities, 'chan', split_axis=0, concat_axis=2, tiled=T...  25.1 us
    dot_general x8, matrix products, block_terms(): lax.dot_general(left_flat, stacked, (((2,), (2,)), ((1,), (1,))), preferr...  24.4 us
    convert_element_type x8, other arithmetic, block_terms(): (vis_real * right_kern[0][None, None] - vis_imag * right_kern[1][None, No...  21 us
    dot_general x4, matrix products, apply_table(): jnp.einsum('gyu,guq->gyq', table, data, preferred_element_type=jnp.float32)  16.7 us
  transfers between devices with their start and end apart: 2, of which 2 were waited for; matrix products, arithmetic and copies ran while one was open for 1% of the time, Pallas kernels for 0%

commit v1 on v0

--- a/solution.py
+++ b/solution.py
@@ -158,7 +158,7 @@
     col_ids = facet_id * FX + jnp.arange(FX, dtype=jnp.int32)
     image = jnp.zeros((num_chans * num_pols, FY, FX), jnp.float32)
     partial_sum = jnp.dot(plane_pick, grid_parts, precision=lax.Precision.HIGHEST)
-    summed = lax.psum(partial_sum, "facet")
+    summed = jnp.sum(jax.lax.all_gather(partial_sum, axis_name="facet"), axis=0)
     subgrid = summed.reshape(NSUB, 2, side_len, row_width).astype(jnp.bfloat16)
     sub_index = jnp.arange(NSUB, dtype=jnp.int32)
     row_cos, row_sin = row_tables(sub_index, side_len, FY, period)

time: 464 us -> 773 us (1.67)
  waiting for transfers between devices: 30.5 us -> 403 us
  blocking collectives: 104 us -> 0 us
  other arithmetic: 102 us -> 124 us
  between operations: 0.11 us -> 13.5 us
    all_gather x0 -> x1, waiting for transfers between devices: none -> 367 us  [shards(): summed = jnp.sum(jax.lax.all_gather(partial_sum, axis_name='facet'), axis=0)]
    psum x1 -> x0, blocking collectives: 104 us -> none  [shards(): summed = lax.psum(partial_sum, 'facet')]
    reduce_sum x0 -> x1, other arithmetic: none -> 22.4 us  [shards(): summed = jnp.sum(jax.lax.all_gather(partial_sum, axis_name='facet'), axis=0)]
  transfers between devices with their start and end apart: 2 -> 3, of which waited for: 2 -> 3; matrix products, arithmetic and copies ran while one was open for 1% -> 1% of each run, Pallas kernels for 0% -> 0%
where the time goes in v1:
time: 773 us; the launch traced here: 770 us
  waiting for transfers between devices  403 us (52%)
  other arithmetic  124 us (16%)
  local copies, waits for them, and re-layouts  116 us (15%)
  matrix products  88.1 us (11%)
  loops' own time  17.9 us (2%)
  between operations  13.5 us (2%)
  starting transfers between devices  8.02 us (1%)
    all_gather x1, waiting for transfers between devices, shards(): summed = jnp.sum(jax.lax.all_gather(partial_sum, axis_name='facet'), axis=0)  367 us
    while x56, local copies, waits for them, and re-layouts  38.8 us
    dot_general x4, matrix products, add_group(): jnp.einsum('grycv,grvx->cyx', row_piece, col_table, preferred_element_typ...  37 us
    convert_element_type x4, other arithmetic, col_tables(): jnp.cos(radians).astype(jnp.bfloat16)  35.7 us
    all_to_all x1, waiting for transfers between devices, shards(): lax.all_to_all(visibilities, 'chan', split_axis=0, concat_axis=2, tiled=T...  27.1 us
    dot_general x8, matrix products, block_terms(): lax.dot_general(left_flat, stacked, (((2,), (2,)), ((1,), (1,))), preferr...  24.4 us
    reduce_sum x1, other arithmetic, shards(): summed = jnp.sum(jax.lax.all_gather(partial_sum, axis_name='facet'), axis=0)  22.4 us
    convert_element_type x8, other arithmetic, block_terms(): (vis_real * right_kern[0][None, None] - vis_imag * right_kern[1][None, No...  21 us
  transfers between devices with their start and end apart: 3, of which 3 were waited for; matrix products, arithmetic and copies ran while one was open for 1% of the time, Pallas kernels for 0%

profile of v1, /device:TPU:2, one launch (start us, length us, event | category | flops | bytes accessed | tf_op | source)
XLA Modules:
  0.0 770.2 jit_solution(5021690877551120553)
XLA Ops:
  6.5 4.6 all-to-all-start
  11.3 27.1 %all-to-all-done = bf16[32,8,1,4096]{3,1,2,0:T(8,128)(2,1)S(1)} async-done(((bf16[32,8,1,4096]{3,1,2,0:T(8,128)(2,1)}), bf16[32,8,1,4096]{3,1,2,0:T(8,128)(2,1)S(1)}, u32[]{:S(2)}, u32[]{:S(2)}) %all-to-all-start) | async-done | bytes 2097184 | tf_op jit(solution)/shard_map/all_to_all | solution.py:133
  38.4 177.2 %while.27 = (s32[]{:T(128)}, f32[8,8,2,32,512]{4,3,2,1,0:T(8,128)}, s32[8]{0:T(128)S(1)}, s32[8,4096]{1,0:T(8,128)}, bf16[32,2,8]{0,2,1:T(8,128)(2,1)S(1)}, /*in...) while((s32[]{:T(128)}, f32[8,8,2,32,512]{4,3,2,1,0:T(8,128)}, ...), condition=%wide.region_1.2_spmd, body=%wide.region_0.1_spmd.sunk | while | flops 587988992 | bytes 84559544 | solution.py:148
  215.5 9.4 %reshape.590 = f32[64,32768]{1,0:T(8,128)} reshape(f32[8,8,2,32,512]{4,3,2,1,0:T(8,128)} %get-tuple-element.178) | data formatting | bytes 16777216 | tf_op jit(solution)/shard_map/reshape | solution.py:150
  224.9 8.4 %fusion.60 = f32[32,32768]{1,0:T(8,128)} fusion(f32[64,32768]{1,0:T(8,128)} %reshape.590, s32[64]{0:T(128)S(1)} %eq.182), kind=kOutput, calls=%fused_computation.121 | convolution fusion | flops 805308416 | bytes 12583168 | tf_op jit(solution)/shard_map/dot_general | solution.py:160
  235.4 367.2 %all-gather.3.cloned.1.call-done = f32[512,32768]{1,0:T(8,128)} async-done(((f32[32,32768]{1,0:T(8,128)}), f32[512,32768]{1,0:T(8,128)}) %all-gather.3.cloned.1.call-update) | async-done | bytes 67108880 | tf_op jit(solution)/shard_map/all_gather | solution.py:161
  602.6 22.4 %reduce_sum.18 = bf16[32,32768]{1,0:T(8,128)(2,1)} reduce(f32[16,32,32768]{2,1,0:T(8,128)} %bitcast.17, f32[]{:T(128)} %constant.223.clone.1), dimensions={0}, to_apply=%region_2.3 | reduce | flops 15728640 | bytes 69206016 | tf_op jit(solution)/shard_map/reduce_sum | solution.py:161
  630.1 4.0 fusion.56
  634.2 4.2 convolution_subtract_fusion
  638.4 6.8 copy.35
  645.2 5.7 convolution_add_fusion
  650.9 6.9 copy.36
  657.9 9.8 %fusion.54 = bf16[32,2,64,16,32]{2,4,3,0,1:T(8,128)(2,1)} fusion(f32[32,1,64,16,32]{2,4,3,0,1:T(8,128)} %bitcast.142, f32[32,1,64,16,32]{2,4,3,0,1:T(8,128)} %bitcast.141), kind=kLoop, calls=%fused_computation.97 | loop fusion | flops 6291456 | bytes 12582912 | tf_op jit(solution)/shard_map/convert_element_type | solution.py:108
  667.7 73.2 %while.28 = (s32[]{:T(128)}, f32[16,64,2048]{2,1,0:T(8,128)}, bf16[32,2,64,16,32]{2,4,3,0,1:T(8,128)(2,1)}, s32[]{:T(128)}, s32[]{:T(128)}, /*index=5*/s32[]{:T(128)}, s32[]{:T(128)}, s32[]{:T(128)}) while((s32[]{:T(128)}, f32[16,64,2048]{2,1,0:T(8,128)}, bf16[32,2,64,16,32]{2,4,3,0,1:T(8,128)(2,1)}, s32[]{:T(128)}, s32[]{:T(128)}, ...), condition=%wide.region_4.5_spmd.clone, body=%wide.region_3.4_spmd.clone.sunk | while | flops 2164789760 | bytes 23087320 | solution.py:127
  667.8 8.9 %cosine_convert_fusion.5 = (bf16[8,1,32,2048]{3,2,1,0:T(8,128)(2,1)S(1)}, bf16[8,1,32,2048]{3,2,1,0:T(8,128)(2,1)S(1)}) fusion(s32[2048]{0:T(1024)S(1)} %add_add_fusion.2, s32[8,32]{1,0:T(8,128)S(1)} %iota_add_fusion.4), kind=kLoop, calls=%fused_computation.85.clone.1 | loop fusion | flops 8912896 | bytes 2106368 | tf_op jit(solution)/shard_map/while/body/eval_jaxpr/convert_element_type | solution.py:44
  676.7 7.4 bitcast_add_fusion.2
  684.3 8.9 %cosine_convert_fusion.5 = (bf16[8,1,32,2048]{3,2,1,0:T(8,128)(2,1)S(1)}, bf16[8,1,32,2048]{3,2,1,0:T(8,128)(2,1)S(1)}) fusion(s32[2048]{0:T(1024)S(1)} %add_add_fusion.2, s32[8,32]{1,0:T(8,128)S(1)} %iota_add_fusion.4), kind=kLoop, calls=%fused_computation.85.clone.1 | loop fusion | flops 8912896 | bytes 2106368 | tf_op jit(solution)/shard_map/while/body/eval_jaxpr/convert_element_type | solution.py:44
  693.2 9.9 %bitcast_add_fusion.2 = f32[16,64,2048]{2,1,0:T(8,128)} fusion(f32[16,64,2048]{2,1,0:T(8,128)} %get-tuple-element.474, pred[]{:T(512)S(6)} %compare.19, bf16[8,1,32,2048]{3,2,1,0:T(8,128)(2,1)S(1)} %get-tuple-element.430, bf16[8,1,32,2048]{3,2,1,0:T(8,128)(2,1)S(1)} %get-tuple-element.431, bf16[32,2,64,16,32]{2,4,3,0,1:T(8,128)(2,1)} %get-tuple-element.483, ...), kind=kOutput, calls=%fused_computation.71.clone.1 | convolution fusion | flops 2155872256 | bytes 20971524 | tf_op jit(solution)/shard_map/while/body/eval_jaxpr/grycv,grvx->cyx/dot_general | solution.py:123
  703.2 8.9 %cosine_convert_fusion.5 = (bf16[8,1,32,2048]{3,2,1,0:T(8,128)(2,1)S(1)}, bf16[8,1,32,2048]{3,2,1,0:T(8,128)(2,1)S(1)}) fusion(s32[2048]{0:T(1024)S(1)} %add_add_fusion.2, s32[8,32]{1,0:T(8,128)S(1)} %iota_add_fusion.4), kind=kLoop, calls=%fused_computation.85.clone.1 | loop fusion | flops 8912896 | bytes 2106368 | tf_op jit(solution)/shard_map/while/body/eval_jaxpr/convert_element_type | solution.py:44
  712.1 9.9 %bitcast_add_fusion.2 = f32[16,64,2048]{2,1,0:T(8,128)} fusion(f32[16,64,2048]{2,1,0:T(8,128)} %get-tuple-element.474, pred[]{:T(512)S(6)} %compare.19, bf16[8,1,32,2048]{3,2,1,0:T(8,128)(2,1)S(1)} %get-tuple-element.430, bf16[8,1,32,2048]{3,2,1,0:T(8,128)(2,1)S(1)} %get-tuple-element.431, bf16[32,2,64,16,32]{2,4,3,0,1:T(8,128)(2,1)} %get-tuple-element.483, ...), kind=kOutput, calls=%fused_computation.71.clone.1 | convolution fusion | flops 2155872256 | bytes 20971524 | tf_op jit(solution)/shard_map/while/body/eval_jaxpr/grycv,grvx->cyx/dot_general | solution.py:123
  722.1 8.9 %cosine_convert_fusion.5 = (bf16[8,1,32,2048]{3,2,1,0:T(8,128)(2,1)S(1)}, bf16[8,1,32,2048]{3,2,1,0:T(8,128)(2,1)S(1)}) fusion(s32[2048]{0:T(1024)S(1)} %add_add_fusion.2, s32[8,32]{1,0:T(8,128)S(1)} %iota_add_fusion.4), kind=kLoop, calls=%fused_computation.85.clone.1 | loop fusion | flops 8912896 | bytes 2106368 | tf_op jit(solution)/shard_map/while/body/eval_jaxpr/convert_element_type | solution.py:44
  731.0 9.9 %bitcast_add_fusion.2 = f32[16,64,2048]{2,1,0:T(8,128)} fusion(f32[16,64,2048]{2,1,0:T(8,128)} %get-tuple-element.474, pred[]{:T(512)S(6)} %compare.19, bf16[8,1,32,2048]{3,2,1,0:T(8,128)(2,1)S(1)} %get-tuple-element.430, bf16[8,1,32,2048]{3,2,1,0:T(8,128)(2,1)S(1)} %get-tuple-element.431, bf16[32,2,64,16,32]{2,4,3,0,1:T(8,128)(2,1)} %get-tuple-element.483, ...), kind=kOutput, calls=%fused_computation.71.clone.1 | convolution fusion | flops 2155872256 | bytes 20971524 | tf_op jit(solution)/shard_map/while/body/eval_jaxpr/grycv,grvx->cyx/dot_general | solution.py:123
  749.2 8.4 %collective-permute-done = f32[16,64,128]{2,1,0:T(8,128)S(1)} collective-permute-done((f32[16,64,128]{2,1,0:T(8,128)S(1)}, f32[16,64,128]{2,1,0:T(8,128)S(1)}, u32[]{:S(2)}, u32[]{:S(2)}) %collective-permute-start) | collective-permute-done | bytes 524320 | tf_op jit(solution)/shard_map/ppermute | solution.py:18
  758.7 4.6 pad_maximum_fusion
  (239 shorter events, 176.4 us)
Async XLA Ops:
  6.5 228.7 %copy-start = (s32[16,32]{1,0:T(8,128)S(1)}, s32[16,32]{1,0:T(8,128)}, u32[]{:S(2)}) copy-start(s32[16,32]{1,0:T(8,128)} %param.16) | copy-start | bytes 6148
  6.5 4.7 copy-start.2
  6.5 31.8 %copy-start.1 = (bf16[32,2,8]{0,2,1:T(8,128)(2,1)S(1)}, bf16[32,2,8]{0,2,1:T(8,128)(2,1)}, u32[]{:S(2)}) copy-start(bf16[32,2,8]{0,2,1:T(8,128)(2,1)} %param.12) | copy-start | bytes 3076
  6.5 31.8 %all-to-all-start = ((bf16[32,8,1,4096]{3,1,2,0:T(8,128)(2,1)}), bf16[32,8,1,4096]{3,1,2,0:T(8,128)(2,1)S(1)}, u32[]{:S(2)}, u32[]{:S(2)}) async-start(bf16[32,8,1,4096]{3,1,2,0:T(8,128)(2,1)} %param.11), calls=%async_computation | async-start | bytes 4194304 | tf_op jit(solution)/shard_map/all_to_all | solution.py:133
  11.1 591.5 %all-gather.3.cloned.1.call-start = ((), (), s32[]{:S(2)}) async-start(), calls=%async_computation.1 | async-start | bytes 71303168 | tf_op jit(solution)/shard_map/all_gather | solution.py:161
  233.4 0.7 copy-start.3
  742.0 15.6 %collective-permute-start = (f32[16,64,128]{2,1,0:T(8,128)S(1)}, f32[16,64,128]{2,1,0:T(8,128)S(1)}, u32[]{:S(2)}, u32[]{:S(2)}) collective-permute-start(f32[16,64,128]{2,1,0:T(8,128)S(1)} %slice_multiply_fusion), channel_id=1, source_target_pairs={{0,1},{1,2},{2,3},{3,4},{4,5},{5,6},{6,7},{7,8},{8,9},{9,10},{10,1... | collective-permute-start | bytes 1572872 | tf_op jit(solution)/shard_map/ppermute | solution.py:18
Sparse Core Ops, SparseCore 0:
  233.5 369.0 all-gather.2
